TPU v7x, 32 devices: a whole 2x2x4 slice. The times are simulated.
32 devices in a mesh: group: 4 (over y, x), dom: 4 (over z), sub: 2 (over core).
Axes of the slice: x: 2, y: 2, z: 4, core: 2. Of those that a mesh axis runs over, the one named last changes fastest.
Arguments:
- fourier: float32 [1152, 4, 64, 16], P('dom', None, ('group', 'sub')), may hold values from -6 to 6
- legendre: float32 [8, 1152, 640], P('dom'), may hold values from -0.1875 to 0.1875
- eta_start: float32 [128, 512], P(('group', 'sub'), 'dom'), may hold values from -6 to 6
- coefs: float32 [9, 128, 512], P(None, ('group', 'sub'), 'dom'), may hold values from 0.1 to 1
- wet: int32 [128, 512], P(('group', 'sub'), 'dom'), may hold values 0 or 1
- src_index: int32 [128, 4, 2], P(('group', 'sub'), 'dom'), may hold values from 0 to 143
- regrid_weight: float32 [128, 4, 2, 128, 128], P(('group', 'sub'), 'dom'), may hold values from -0.375 to 0.375
Outputs:
- spectral: float32 [8, 4, 64, 2, 640], P('dom', None, ('group', 'sub'))
- eta_final: float32 [128, 512], P(('group', 'sub'), 'dom')
All inputs are finite; a program needn't handle non-finite values. No bound on the sum of `wet` on one device may be relied on, other than what follows from the above.
Results may differ from a plain program's by a relative error of at most 0.00011.
Values sent between devices are 32-bit elements; how exact they have to be, the bound alone decides.
A program may use at most 64 MiB of HBM per device.

v0:
```python
import jax
import jax.numpy as jnp
from jax import lax
from jax.sharding import PartitionSpec as P

SUBS = 8


forcing_rate = 0.5


def padded(cells, sides, width):
    for axis, dim in sides:
        count = lax.axis_size(axis)
        ends = count - 1
        head = lax.slice_in_dim(cells, 0, width, axis=dim)
        tail = lax.slice_in_dim(cells, cells.shape[dim] - width, cells.shape[dim], axis=dim)
        cells = jnp.concatenate(
            [
                lax.ppermute(tail, axis, [(i, (i + 1) % count) for i in range(ends)]),
                cells,
                lax.ppermute(head, axis, [((i + 1) % count, i) for i in range(ends)]),
            ],
            axis=dim,
        )
    return cells


def relax(extended, table):
    rows_out = extended.shape[0] - 2
    cols_out = extended.shape[1] - 2
    total = table[0] * extended[0:rows_out, 0:cols_out]
    for index in range(1, 9):
        shift_row = index // 3
        shift_col = index % 3
        total = (
            total
            + table[index]
            * extended[shift_row : shift_row + rows_out, shift_col : shift_col + cols_out]
        )
    return table[9] * (total + forcing_rate * table[10])


def widen(eta, width):
    return padded(eta, ((("group", "sub"), 0), ("dom", 1)), width)


def body(fourier, legendre, eta_start, coefs, wet, src_index, regrid_weight):
    lev_dev = fourier.shape[2]
    m_dev = legendre.shape[0]
    block = lax.all_to_all(fourier, "dom", split_axis=3, concat_axis=0, tiled=True)
    parts = block.reshape(block.shape[0], block.shape[1], lev_dev, m_dev, 2)
    spectral = jnp.einsum("man,avlmr->mvlrn", legendre, parts, precision=lax.Precision.HIGHEST)
    rows_dev = eta_start.shape[0]
    blocks = eta_start.shape[1]
    surface = fourier[:, 0, 0, :]
    flux = surface.reshape(1, surface.shape[0] * surface.shape[1] // blocks, blocks)
    piece = lax.all_gather(flux, "dom", axis=1, tiled=True)
    count = piece.shape[1]
    labels = lax.iota(jnp.int32, count)
    onehot = (src_index[..., None] == labels).astype(jnp.float32)
    picked = jnp.einsum("rdkp,ps->rdks", onehot, piece[0], precision=lax.Precision.HIGHEST)
    forcing = jnp.einsum("rdkts,rdks->rdt", regrid_weight, picked, precision=lax.Precision.HIGHEST)
    forcing = forcing.reshape(rows_dev, blocks)
    norm = coefs / jnp.sum(coefs, axis=0)
    stacked = jnp.concatenate([norm, wet.astype(jnp.float32)[None], forcing[None]], axis=0)
    width = 4
    margin = 3
    table = padded(stacked, ((("group", "sub"), 1), ("dom", 2)), 3)
    eta = eta_start
    for outer in range(SUBS // width):
        extended = widen(eta, width)
        for inner in range(width):
            inset = width - inner - 1
            first = margin - inset
            region = table[
                :, first : first + rows_dev + 2 * inset, first : first + blocks + 2 * inset
            ]
            extended = relax(extended, region)
        eta = extended
    return (spectral, eta)


def solution(mesh):
    placed = (
        P("dom", None, ("group", "sub"), None),
        P("dom", None, None),
        P(("group", "sub"), "dom"),
        P(None, ("group", "sub"), "dom"),
        P(("group", "sub"), "dom"),
        P(("group", "sub"), "dom", None),
        P(("group", "sub"), "dom", None, None, None),
    )
    return jax.shard_map(
        body,
        mesh=mesh,
        in_specs=placed,
        out_specs=(P("dom", None, ("group", "sub"), None, None), P(("group", "sub"), "dom")),
        check_vma=False,
    )
```

profile of v0, /device:TPU:0, one launch (start us, length us, event | category | flops | bytes accessed | tf_op | source)
XLA Modules:
  0.0 95.5 jit_solution(11806278115259470243)
XLA Ops:
  0.6 0.0 copy-start
  0.6 0.0 copy-start.2
  0.7 0.9 fusion.94
  1.5 1.3 %collective-permute-start.5 = (f32[4,128]{1,0:T(4,128)S(1)}, f32[4,128]{1,0:T(4,128)S(1)}, u32[]{:S(2)}, u32[]{:S(2)}) collective-permute-start(f32[4,128]{1,0:T(4,128)S(1)} %get-tuple-element.19), channel_id=1, source_target_pairs={{1,0},{8,1},{9,8},{16,9},{17,16},{24,17},{25,24},{3,2},{10,3},{11,... | collective-permute-start | bytes 6152 | tf_op jit(solution)/shard_map/ppermute | solution.py:22
  2.8 3.0 %collective-permute-start.4 = (f32[4,128]{1,0:T(4,128)S(1)}, f32[4,128]{1,0:T(4,128)S(1)}, u32[]{:S(2)}, u32[]{:S(2)}) collective-permute-start(f32[4,128]{1,0:T(4,128)S(1)} %get-tuple-element.18), channel_id=1, source_target_pairs={{0,1},{1,8},{8,9},{9,16},{16,17},{17,24},{24,25},{2,3},{3,10},{10,... | collective-permute-start | bytes 6152 | tf_op jit(solution)/shard_map/ppermute | solution.py:20
  5.8 0.7 slice.450
  6.6 0.1 copy.19
  6.7 0.1 reshape_squeeze.4
  6.8 15.0 %all_gather.3 = f32[1,144,128]{2,0,1:T(1,128)S(1)} all-gather(f32[1,36,128]{2,0,1:T(1,128)S(1)} %reshape_squeeze.4), channel_id=1, replica_groups=mesh['group'=4,'dom'=4,'sub'=2] {'dom'}, dimensions={1}, use_global_device_ids=true | all-gather | bytes 92160 | tf_op jit(solution)/shard_map/all_gather | solution.py:58
  21.8 0.7 convert_bitcast_fusion
  22.5 0.9 reduce_sum.9
  23.4 0.0 copy-start.1
  23.4 1.0 %broadcast_divide_fusion = f32[9,16,128]{2,1,0:T(8,128)S(1)} fusion(f32[9,16,128]{2,1,0:T(8,128)} %param.10, f32[16,128]{1,0:T(8,128)S(1)} %reduce_sum.9), kind=kLoop, calls=%fused_computation.9 | loop fusion | flops 18432 | bytes 155648 | tf_op jit(solution)/shard_map/div | solution.py:65
  24.4 0.9 convolution_bitcast_fusion
  25.3 0.0 copy-done
  25.3 1.8 %fusion.2 = f32[16,1,128,1]{2,1,3,0:T(1,128)S(1)} fusion(f32[16,1,2,128,128]{4,3,2,1,0:T(8,128)S(1)} %copy-done, f32[16,2,128,1]{2,0,1,3:T(8,128)S(1)} %convolution_bitcast_fusion), kind=kOutput, calls=%fused_computation.2 | convolution fusion | flops 6291456 | bytes 2121728 | tf_op jit(solution)/shard_map/rdkts,rdks->rdt/dot_general | solution.py:63
  27.1 1.3 %collective-permute-start.1 = (f32[11,3,128]{2,1,0:T(4,128)S(1)}, f32[11,3,128]{2,1,0:T(4,128)S(1)}, u32[]{:S(2)}, u32[]{:S(2)}) collective-permute-start(f32[11,3,128]{2,1,0:T(4,128)S(1)} %get-tuple-element.11), channel_id=1, source_target_pairs={{1,0},{8,1},{9,8},{16,9},{17,16},{24,17},{25,24},{3,2},{10,3},{11,... | collective-permute-start | bytes 50696 | tf_op jit(solution)/shard_map/ppermute | solution.py:22
  28.4 3.0 %collective-permute-start = (f32[11,3,128]{2,1,0:T(4,128)S(1)}, f32[11,3,128]{2,1,0:T(4,128)S(1)}, u32[]{:S(2)}, u32[]{:S(2)}) collective-permute-start(f32[11,3,128]{2,1,0:T(4,128)S(1)} %get-tuple-element.10), channel_id=1, source_target_pairs={{0,1},{1,8},{8,9},{9,16},{16,17},{17,24},{24,25},{2,3},{3,10},{10,... | collective-permute-start | bytes 50696 | tf_op jit(solution)/shard_map/ppermute | solution.py:20
  31.5 0.0 collective-permute-done.5
  31.5 0.0 collective-permute-done.4
  31.5 0.7 pad_maximum_fusion.7
  32.2 0.1 fusion.92
  32.3 1.3 %collective-permute-start.7 = (f32[24,4]{1,0:T(8,128)S(1)}, f32[24,4]{1,0:T(8,128)S(1)}, u32[]{:S(2)}, u32[]{:S(2)}) collective-permute-start(f32[24,4]{1,0:T(8,128)S(1)} %get-tuple-element.15), channel_id=1, source_target_pairs={{2,0},{4,2},{6,4},{3,1},{5,3},{7,5},{10,8},{12,10},{14,12},{11,9},... | collective-permute-start | bytes 1160 | tf_op jit(solution)/shard_map/ppermute | solution.py:22
  33.6 4.5 %collective-permute-start.6 = (f32[24,4]{1,0:T(8,128)S(1)}, f32[24,4]{1,0:T(8,128)S(1)}, u32[]{:S(2)}, u32[]{:S(2)}) collective-permute-start(f32[24,4]{1,0:T(8,128)S(1)} %get-tuple-element.14), channel_id=1, source_target_pairs={{0,2},{2,4},{4,6},{1,3},{3,5},{5,7},{8,10},{10,12},{12,14},{9,11},... | collective-permute-start | bytes 1160 | tf_op jit(solution)/shard_map/ppermute | solution.py:20
  38.1 0.0 collective-permute-done.1
  38.1 0.0 collective-permute-done
  38.2 0.1 fusion.90
  38.3 1.3 %collective-permute-start.3 = (f32[11,22,3]{2,1,0:T(8,128)S(1)}, f32[11,22,3]{2,1,0:T(8,128)S(1)}, u32[]{:S(2)}, u32[]{:S(2)}) collective-permute-start(f32[11,22,3]{2,1,0:T(8,128)S(1)} %get-tuple-element.9), channel_id=1, source_target_pairs={{2,0},{4,2},{6,4},{3,1},{5,3},{7,5},{10,8},{12,10},{14,12},{11,9},... | collective-permute-start | bytes 8720 | tf_op jit(solution)/shard_map/ppermute | solution.py:22
  39.6 4.6 %collective-permute-start.2 = (f32[11,22,3]{2,1,0:T(8,128)S(1)}, f32[11,22,3]{2,1,0:T(8,128)S(1)}, u32[]{:S(2)}, u32[]{:S(2)}) collective-permute-start(f32[11,22,3]{2,1,0:T(8,128)S(1)} %get-tuple-element.8), channel_id=1, source_target_pairs={{0,2},{2,4},{4,6},{1,3},{3,5},{5,7},{8,10},{10,12},{12,14},{9,11},... | collective-permute-start | bytes 8720 | tf_op jit(solution)/shard_map/ppermute | solution.py:20
  44.1 0.0 collective-permute-done.7
  44.1 0.0 collective-permute-done.6
  44.1 0.8 pad_maximum_fusion.2
  44.9 1.3 %collective-permute-done.3 = f32[11,22,3]{2,1,0:T(8,128)S(1)} collective-permute-done((f32[11,22,3]{2,1,0:T(8,128)S(1)}, f32[11,22,3]{2,1,0:T(8,128)S(1)}, u32[]{:S(2)}, u32[]{:S(2)}) %collective-permute-start.3) | collective-permute-done | bytes 2936 | tf_op jit(solution)/shard_map/ppermute | solution.py:22
  46.2 1.2 %collective-permute-done.2 = f32[11,22,3]{2,1,0:T(8,128)S(1)} collective-permute-done((f32[11,22,3]{2,1,0:T(8,128)S(1)}, f32[11,22,3]{2,1,0:T(8,128)S(1)}, u32[]{:S(2)}, u32[]{:S(2)}) %collective-permute-start.2) | collective-permute-done | bytes 2936 | tf_op jit(solution)/shard_map/ppermute | solution.py:20
  47.4 0.2 pad_maximum_fusion
  47.6 0.1 fusion.60
  47.7 0.2 fusion.49
  47.9 0.2 fusion.38
  48.1 0.0 copy-done.2
  48.1 0.1 fusion.82
  48.2 1.3 %collective-permute-start.9 = (f32[4,128]{1,0:T(4,128)S(1)}, f32[4,128]{1,0:T(4,128)S(1)}, u32[]{:S(2)}, u32[]{:S(2)}) collective-permute-start(f32[4,128]{1,0:T(4,128)S(1)} %get-tuple-element.17), channel_id=1, source_target_pairs={{1,0},{8,1},{9,8},{16,9},{17,16},{24,17},{25,24},{3,2},{10,3},{11,... | collective-permute-start | bytes 6152 | tf_op jit(solution)/shard_map/ppermute | solution.py:22
  49.5 3.0 %collective-permute-start.8 = (f32[4,128]{1,0:T(4,128)S(1)}, f32[4,128]{1,0:T(4,128)S(1)}, u32[]{:S(2)}, u32[]{:S(2)}) collective-permute-start(f32[4,128]{1,0:T(4,128)S(1)} %get-tuple-element.16), channel_id=1, source_target_pairs={{0,1},{1,8},{8,9},{9,16},{16,17},{17,24},{24,25},{2,3},{3,10},{10,... | collective-permute-start | bytes 6152 | tf_op jit(solution)/shard_map/ppermute | solution.py:20
  52.5 0.0 collective-permute-done.9
  52.6 0.8 collective-permute-done.8
  53.4 0.1 fusion.91
  53.4 1.3 %collective-permute-start.11 = (f32[24,4]{1,0:T(8,128)S(1)}, f32[24,4]{1,0:T(8,128)S(1)}, u32[]{:S(2)}, u32[]{:S(2)}) collective-permute-start(f32[24,4]{1,0:T(8,128)S(1)} %get-tuple-element.13), channel_id=1, source_target_pairs={{2,0},{4,2},{6,4},{3,1},{5,3},{7,5},{10,8},{12,10},{14,12},{11,9},... | collective-permute-start | bytes 1160 | tf_op jit(solution)/shard_map/ppermute | solution.py:22
  54.7 5.0 %collective-permute-start.10 = (f32[24,4]{1,0:T(8,128)S(1)}, f32[24,4]{1,0:T(8,128)S(1)}, u32[]{:S(2)}, u32[]{:S(2)}) collective-permute-start(f32[24,4]{1,0:T(8,128)S(1)} %get-tuple-element.12), channel_id=1, source_target_pairs={{0,2},{2,4},{4,6},{1,3},{3,5},{5,7},{8,10},{10,12},{12,14},{9,11},... | collective-permute-start | bytes 1160 | tf_op jit(solution)/shard_map/ppermute | solution.py:20
  59.7 0.0 copy-done.1
  59.8 1.1 %copy.16 = f32[288,4,8,16]{0,2,1,3:T(8,128)} copy(f32[288,4,8,16]{0,3,2,1:T(8,128)S(1)} %copy-done.1) | data formatting | bytes 1179648 | tf_op args[0]
  60.9 4.2 %all-to-all-start = ((f32[288,4,8,16]{0,2,1,3:T(8,128)}), f32[288,4,8,16]{0,2,1,3:T(8,128)S(1)}, u32[]{:S(2)}, u32[]{:S(2)}) async-start(f32[288,4,8,16]{0,2,1,3:T(8,128)} %copy.16), calls=%async_computation | async-start | bytes 1572864 | tf_op jit(solution)/shard_map/all_to_all | solution.py:51
  65.1 0.0 collective-permute-done.11
  65.1 0.0 collective-permute-done.10
  65.1 0.1 pad_maximum_fusion.3
  65.2 0.1 fusion.27
  65.3 0.2 fusion.17
  65.5 0.2 fusion.7
  65.7 0.7 fusion.72
  66.4 19.9 %all-to-all-done = f32[288,4,8,16]{0,2,1,3:T(8,128)S(1)} async-done(((f32[288,4,8,16]{0,2,1,3:T(8,128)}), f32[288,4,8,16]{0,2,1,3:T(8,128)S(1)}, u32[]{:S(2)}, u32[]{:S(2)}) %all-to-all-start) | async-done | bytes 589856 | tf_op jit(solution)/shard_map/all_to_all | solution.py:51
  86.3 1.4 %copy.30 = f32[288,4,8,4,4]{0,3,2,4,1:T(4,128)} copy(f32[288,4,8,4,4]{0,2,1,4,3:T(8,128)S(1)} %bitcast.283) | data formatting | bytes 1179648 | tf_op jit(solution)/shard_map/all_to_all | solution.py:51
  87.7 1.5 %reshape.30 = f32[1152,4,8,2,2]{0,2,4,3,1:T(8,128)S(1)} reshape(f32[4,288,4,8,4]{1,0,3,4,2:T(4,128)} %bitcast.284) | data formatting | bytes 1179648 | tf_op jit(solution)/shard_map/reshape | solution.py:52
  89.2 5.3 %fusion = f32[2,4,8,2,640]{4,2,3,1,0:T(8,128)S(1)} fusion(f32[2,1152,640]{2,1,0:T(8,128)} %param.8, f32[1152,4,8,2,2]{0,2,4,3,1:T(8,128)S(1)} %reshape.30), kind=kOutput, calls=%fused_computation | convolution fusion | flops 1132462080 | bytes 6815744 | tf_op jit(solution)/shard_map/man,avlmr->mvlrn/dot_general | solution.py:53
  94.6 0.9 copy.21
  (4 shorter events, 0.1 us)
Async XLA Ops:
  0.6 24.6 %copy-start = (f32[16,1,2,128,128]{4,3,2,1,0:T(8,128)S(1)}, f32[16,1,2,128,128]{4,3,2,1,0:T(8,128)}, u32[]{:S(2)}) copy-start(f32[16,1,2,128,128]{4,3,2,1,0:T(8,128)} %param.13) | copy-start | bytes 6291460
  0.6 47.5 %copy-start.2 = (s32[16,128]{1,0:T(8,128)S(1)}, s32[16,128]{1,0:T(8,128)}, u32[]{:S(2)}) copy-start(s32[16,128]{1,0:T(8,128)} %param.11) | copy-start | bytes 24580
  1.5 29.9 %collective-permute-start.5 = (f32[4,128]{1,0:T(4,128)S(1)}, f32[4,128]{1,0:T(4,128)S(1)}, u32[]{:S(2)}, u32[]{:S(2)}) collective-permute-start(f32[4,128]{1,0:T(4,128)S(1)} %get-tuple-element.19), channel_id=1, source_target_pairs={{1,0},{8,1},{9,8},{16,9},{17,16},{24,17},{25,24},{3,2},{10,3},{11,... | collective-permute-start | bytes 6152 | tf_op jit(solution)/shard_map/ppermute | solution.py:22
  2.8 28.7 %collective-permute-start.4 = (f32[4,128]{1,0:T(4,128)S(1)}, f32[4,128]{1,0:T(4,128)S(1)}, u32[]{:S(2)}, u32[]{:S(2)}) collective-permute-start(f32[4,128]{1,0:T(4,128)S(1)} %get-tuple-element.18), channel_id=1, source_target_pairs={{0,1},{1,8},{8,9},{9,16},{16,17},{17,24},{24,25},{2,3},{3,10},{10,... | collective-permute-start | bytes 6152 | tf_op jit(solution)/shard_map/ppermute | solution.py:20
  23.4 36.4 %copy-start.1 = (f32[288,4,8,16]{0,3,2,1:T(8,128)S(1)}, f32[288,4,8,16]{0,3,2,1:T(8,128)}, u32[]{:S(2)}) copy-start(f32[288,4,8,16]{0,3,2,1:T(8,128)} %param.7) | copy-start | bytes 1769476
  27.1 11.0 %collective-permute-start.1 = (f32[11,3,128]{2,1,0:T(4,128)S(1)}, f32[11,3,128]{2,1,0:T(4,128)S(1)}, u32[]{:S(2)}, u32[]{:S(2)}) collective-permute-start(f32[11,3,128]{2,1,0:T(4,128)S(1)} %get-tuple-element.11), channel_id=1, source_target_pairs={{1,0},{8,1},{9,8},{16,9},{17,16},{24,17},{25,24},{3,2},{10,3},{11,... | collective-permute-start | bytes 50696 | tf_op jit(solution)/shard_map/ppermute | solution.py:22
  28.4 9.7 %collective-permute-start = (f32[11,3,128]{2,1,0:T(4,128)S(1)}, f32[11,3,128]{2,1,0:T(4,128)S(1)}, u32[]{:S(2)}, u32[]{:S(2)}) collective-permute-start(f32[11,3,128]{2,1,0:T(4,128)S(1)} %get-tuple-element.10), channel_id=1, source_target_pairs={{0,1},{1,8},{8,9},{9,16},{16,17},{17,24},{24,25},{2,3},{3,10},{10,... | collective-permute-start | bytes 50696 | tf_op jit(solution)/shard_map/ppermute | solution.py:20
  32.3 11.9 %collective-permute-start.7 = (f32[24,4]{1,0:T(8,128)S(1)}, f32[24,4]{1,0:T(8,128)S(1)}, u32[]{:S(2)}, u32[]{:S(2)}) collective-permute-start(f32[24,4]{1,0:T(8,128)S(1)} %get-tuple-element.15), channel_id=1, source_target_pairs={{2,0},{4,2},{6,4},{3,1},{5,3},{7,5},{10,8},{12,10},{14,12},{11,9},... | collective-permute-start | bytes 1160 | tf_op jit(solution)/shard_map/ppermute | solution.py:22
  33.6 10.6 %collective-permute-start.6 = (f32[24,4]{1,0:T(8,128)S(1)}, f32[24,4]{1,0:T(8,128)S(1)}, u32[]{:S(2)}, u32[]{:S(2)}) collective-permute-start(f32[24,4]{1,0:T(8,128)S(1)} %get-tuple-element.14), channel_id=1, source_target_pairs={{0,2},{2,4},{4,6},{1,3},{3,5},{5,7},{8,10},{10,12},{12,14},{9,11},... | collective-permute-start | bytes 1160 | tf_op jit(solution)/shard_map/ppermute | solution.py:20
  38.3 8.0 %collective-permute-start.3 = (f32[11,22,3]{2,1,0:T(8,128)S(1)}, f32[11,22,3]{2,1,0:T(8,128)S(1)}, u32[]{:S(2)}, u32[]{:S(2)}) collective-permute-start(f32[11,22,3]{2,1,0:T(8,128)S(1)} %get-tuple-element.9), channel_id=1, source_target_pairs={{2,0},{4,2},{6,4},{3,1},{5,3},{7,5},{10,8},{12,10},{14,12},{11,9},... | collective-permute-start | bytes 8720 | tf_op jit(solution)/shard_map/ppermute | solution.py:22
  39.6 7.8 %collective-permute-start.2 = (f32[11,22,3]{2,1,0:T(8,128)S(1)}, f32[11,22,3]{2,1,0:T(8,128)S(1)}, u32[]{:S(2)}, u32[]{:S(2)}) collective-permute-start(f32[11,22,3]{2,1,0:T(8,128)S(1)} %get-tuple-element.8), channel_id=1, source_target_pairs={{0,2},{2,4},{4,6},{1,3},{3,5},{5,7},{8,10},{10,12},{12,14},{9,11},... | collective-permute-start | bytes 8720 | tf_op jit(solution)/shard_map/ppermute | solution.py:20
  48.2 4.3 %collective-permute-start.9 = (f32[4,128]{1,0:T(4,128)S(1)}, f32[4,128]{1,0:T(4,128)S(1)}, u32[]{:S(2)}, u32[]{:S(2)}) collective-permute-start(f32[4,128]{1,0:T(4,128)S(1)} %get-tuple-element.17), channel_id=1, source_target_pairs={{1,0},{8,1},{9,8},{16,9},{17,16},{24,17},{25,24},{3,2},{10,3},{11,... | collective-permute-start | bytes 6152 | tf_op jit(solution)/shard_map/ppermute | solution.py:22
  49.5 3.8 %collective-permute-start.8 = (f32[4,128]{1,0:T(4,128)S(1)}, f32[4,128]{1,0:T(4,128)S(1)}, u32[]{:S(2)}, u32[]{:S(2)}) collective-permute-start(f32[4,128]{1,0:T(4,128)S(1)} %get-tuple-element.16), channel_id=1, source_target_pairs={{0,1},{1,8},{8,9},{9,16},{16,17},{17,24},{24,25},{2,3},{3,10},{10,... | collective-permute-start | bytes 6152 | tf_op jit(solution)/shard_map/ppermute | solution.py:20
  53.4 11.7 %collective-permute-start.11 = (f32[24,4]{1,0:T(8,128)S(1)}, f32[24,4]{1,0:T(8,128)S(1)}, u32[]{:S(2)}, u32[]{:S(2)}) collective-permute-start(f32[24,4]{1,0:T(8,128)S(1)} %get-tuple-element.13), channel_id=1, source_target_pairs={{2,0},{4,2},{6,4},{3,1},{5,3},{7,5},{10,8},{12,10},{14,12},{11,9},... | collective-permute-start | bytes 1160 | tf_op jit(solution)/shard_map/ppermute | solution.py:22
  54.7 10.4 %collective-permute-start.10 = (f32[24,4]{1,0:T(8,128)S(1)}, f32[24,4]{1,0:T(8,128)S(1)}, u32[]{:S(2)}, u32[]{:S(2)}) collective-permute-start(f32[24,4]{1,0:T(8,128)S(1)} %get-tuple-element.12), channel_id=1, source_target_pairs={{0,2},{2,4},{4,6},{1,3},{3,5},{5,7},{8,10},{10,12},{12,14},{9,11},... | collective-permute-start | bytes 1160 | tf_op jit(solution)/shard_map/ppermute | solution.py:20
  60.9 25.4 %all-to-all-start = ((f32[288,4,8,16]{0,2,1,3:T(8,128)}), f32[288,4,8,16]{0,2,1,3:T(8,128)S(1)}, u32[]{:S(2)}, u32[]{:S(2)}) async-start(f32[288,4,8,16]{0,2,1,3:T(8,128)} %copy.16), calls=%async_computation | async-start | bytes 1572864 | tf_op jit(solution)/shard_map/all_to_all | solution.py:51
where the time goes:
time: 96.3 us; the launch traced here: 95.5 us
  starting transfers between devices  35.1 us (36%)
  waiting for transfers between devices  23.2 us (24%)
  blocking collectives  15 us (16%)
  matrix products  8.04 us (8%)
  local copies, waits for them, and re-layouts  6.99 us (7%)
  other arithmetic  6.11 us (6%)
  between operations  0.98 us (1%)
    ppermute x6, starting transfers between devices, padded(): lax.ppermute(tail, axis, [(i, (i + 1) % count) for i in range(ends)])  23.2 us
    all_to_all x1, waiting for transfers between devices, body(): lax.all_to_all(fourier, 'dom', split_axis=3, concat_axis=0, tiled=True)  19.9 us
    all_gather x1, blocking collectives, body(): piece = lax.all_gather(flux, 'dom', axis=1, tiled=True)  15 us
    ppermute x6, starting transfers between devices, padded(): lax.ppermute(head, axis, [((i + 1) % count, i) for i in range(ends)])  7.72 us
    dot_general x1, matrix products, body(): jnp.einsum('man,avlmr->mvlrn', legendre, parts, precision=lax.Precision.H...  5.35 us
    all_to_all x1, starting transfers between devices, body(): lax.all_to_all(fourier, 'dom', split_axis=3, concat_axis=0, tiled=True)  4.22 us
    unnamed x8, local copies, waits for them, and re-layouts  2.04 us
    ppermute x6, waiting for transfers between devices, padded(): lax.ppermute(tail, axis, [(i, (i + 1) % count) for i in range(ends)])  1.98 us
  transfers between devices with their start and end apart: 13, of which 4 were waited for; matrix products, arithmetic and copies ran while one was open for 11% of the time, Pallas kernels for 0%

commit v1 on v0

v1 whole, which is shorter than its diff:
```python
import functools

import jax
import jax.numpy as jnp
from jax import lax
from jax.experimental import pallas as pl
from jax.experimental.pallas import tpu as pltpu
from jax.sharding import PartitionSpec as P

SUBS = 8
RATE = 0.5
MESH = pl.DeviceIdType.MESH
F32 = jnp.float32
BF16 = jnp.bfloat16


def split(x):
    high = x.astype(BF16)
    return high, (x - high.astype(F32)).astype(BF16)


def dot(a, b):
    return jnp.dot(a, b, preferred_element_type=F32)


def kernel(
    dims,
    x_hbm, l_hbm, eta_hbm, coef_hbm, wet_hbm, idx, w_hbm, fl_hbm,
    spec, eta_out,
    xv, xr, lv, wv, flb, sb, rb, lh, ll, th, tl, xt, cx, wx, ex, fx, fl_w, fl_e, pk_w, pk_e, h_w, h_e, nrm,
    lsem, ssem, rsem,
):
    n, rows_n, subs_n, la, pairs, cols, lev, m_dev, rows, count, slot = dims
    width = SUBS
    main = la // 128 * 128
    tail = la - main
    tiles = main // 128
    cdev = 2 * m_dev
    pad = flb.shape[0] // n
    me = lax.axis_index("dom")
    row = lax.axis_index("group") * subs_n + lax.axis_index("sub")

    def at(drow, ddom):
        target = {}
        if drow:
            other = lax.rem(row + rows_n + drow, rows_n)
            target["group"] = other // subs_n
            target["sub"] = lax.rem(other, subs_n)
        if ddom:
            target["dom"] = lax.rem(me + n + ddom, n)
        return target

    locals_ = []

    def fetch(src, dst):
        copy = pltpu.make_async_copy(src, dst, lsem.at[len(locals_)])
        locals_.append(copy)
        copy.start()
        return copy

    remotes = []

    def send(src, dst, target):
        i = len(remotes)
        copy = pltpu.make_async_remote_copy(
            src_ref=src, dst_ref=dst, send_sem=ssem.at[i], recv_sem=rsem.at[i],
            device_id=target, device_id_type=MESH,
        )
        remotes.append(copy)
        copy.start()
        return copy

    barrier = pltpu.get_barrier_semaphore()
    greet = [at(0, r) for r in range(1, n)]
    greet += [at(dr, dd) for dr in (-1, 1) for dd in (-1, 0, 1)]
    for target in greet:
        pl.semaphore_signal(barrier, inc=1, device_id=target, device_id_type=MESH)
    get_c = fetch(coef_hbm, cx.at[:, pl.ds(width, rows), :])
    get_w = fetch(wet_hbm, wx.at[pl.ds(width, rows), :])
    get_e = fetch(eta_hbm, ex.at[pl.ds(width, rows), :])
    get_x = [fetch(x_hbm.at[:, pl.ds(t * 128, 128)], xv.at[t]) for t in range(tiles)]
    if tail:
        get_x.append(fetch(x_hbm.at[:, pl.ds(main, tail)], xr))
    mine = pl.ds(pl.multiple_of(me * pad, 8), pad)
    get_f = fetch(fl_hbm, flb.at[mine, :])
    get_r = fetch(w_hbm, wv)
    get_l = [fetch(l_hbm.at[m], lv.at[m]) for m in range(m_dev)]

    lane = lax.broadcasted_iota(jnp.int32, (1, 128), 1)
    get_c.wait()
    get_w.wait()
    get_e.wait()
    own = pl.ds(width, rows)
    planes = [cx[k, own, :] for k in range(9)] + [wx[own, :].astype(F32), ex[own, :]]
    left = jnp.zeros((rows, 128), F32)
    right = jnp.zeros((rows, 128), F32)
    for p, plane in enumerate(planes):
        here = (lane >= width * p) & (lane < width * (p + 1))
        left = jnp.where(here, pltpu.roll(plane, width * p, 1), left)
        right = jnp.where(here, pltpu.roll(plane, (width * p + width) % 128, 1), right)
    pk_w[...] = left
    pk_e[...] = right

    pl.semaphore_wait(barrier, len(greet))
    top, bottom = pl.ds(0, width), pl.ds(rows - width, width)
    halo_n, halo_s = pl.ds(0, width), pl.ds(width + rows, width)
    get_flux = [send(fl_hbm, flb.at[mine, :], at(0, r)) for r in range(1, n)]
    edges = []
    for src, dst in ((coef_hbm, cx), ):
        edges.append(send(src.at[:, bottom, :], dst.at[:, halo_n, :], at(1, 0)))
        edges.append(send(src.at[:, top, :], dst.at[:, halo_s, :], at(-1, 0)))
    for src, dst in ((wet_hbm, wx), (eta_hbm, ex)):
        edges.append(send(src.at[bottom, :], dst.at[halo_n, :], at(1, 0)))
        edges.append(send(src.at[top, :], dst.at[halo_s, :], at(-1, 0)))
    for src, dst, dd in ((pk_e, h_w, 1), (pk_w, h_e, -1)):
        edges.append(send(src, dst.at[own, :], at(0, dd)))
        edges.append(send(src.at[bottom, :], dst.at[halo_n, :], at(1, dd)))
        edges.append(send(src.at[top, :], dst.at[halo_s, :], at(-1, dd)))

    for copy in get_x:
        copy.wait()
    vars_n = pairs // lev
    if tail:
        xv[tiles] = jnp.concatenate([xr[...], jnp.zeros((xr.shape[0], 128 - tail), F32)], axis=1)

    def pack(dest, store):
        for c in range(cdev):
            where = dest * cdev + c
            for t in range(tiles):
                store(
                    t * cdev * pairs + c * pairs, pairs,
                    xv.at[t][pl.ds(where, pairs, stride=cols), :],
                )
            if tail:
                rest = xv.at[tiles][pl.ds(where, pairs, stride=cols), :]
                total = rest[0:lev]
                for v in range(1, vars_n):
                    total = total + pltpu.roll(rest[v * lev:(v + 1) * lev], slot * v, 1)
                store(tiles * cdev * pairs + c * lev, lev, total)

    def keep(buffer, which):
        def store(first, height, value):
            buffer[which, pl.ds(first, height), :] = value
        return store

    blocks = []
    for r in range(1, n):
        dest = lax.rem(me + r, n)
        pack(dest, keep(sb, r - 1))
        blocks.append(send(sb.at[r - 1], rb.at[me], at(0, r)))
    pack(me, keep(rb, me))

    for copy in get_l:
        copy.wait()
    per = 128 // slot

    def split_legendre(d, carry):
        for m in range(m_dev):
            if main:
                h, l = split(lv[m, pl.ds(pl.multiple_of(d * la, 8), main), :])
                lh[m, d] = h
                ll[m, d] = l
            if tail:
                part = lv[m, pl.ds(pl.multiple_of(d * la + main, 8), tail), :]
                if slot > tail:
                    part = jnp.concatenate([part, jnp.zeros((slot - tail, part.shape[1]), F32)], axis=0)
                h, l = split(part)
                th[m, d] = h
                tl[m, d] = l
        return carry

    lax.fori_loop(0, n, split_legendre, 0)

    get_f.wait()
    for copy in get_flux:
        copy.wait_recv()
    get_r.wait()

    def regrid(i, total):
        part = None
        for k in range(2):
            block = idx[k, i]
            at_row = (block // count) * pad + lax.rem(block, count)
            term = wv[i, k] * flb[pl.ds(at_row, 1), :]
            part = term if part is None else part + term
        return jnp.where(lane == i, jnp.sum(part, axis=1, keepdims=True), total)

    forced = lax.fori_loop(0, rows, regrid, jnp.zeros((128, 128), F32))
    fx[own, :] = forced.T[0:rows]
    up, down = pl.ds(width, width), pl.ds(rows, width)
    force = []
    force.append(send(fx.at[down, :], fx.at[halo_n, :], at(1, 0)))
    force.append(send(fx.at[up, :], fx.at[halo_s, :], at(-1, 0)))
    for dst, dd in ((fl_w, 1), (fl_e, -1)):
        force.append(send(fx.at[own, :], dst.at[own, :], at(0, dd)))
        force.append(send(fx.at[down, :], dst.at[halo_n, :], at(1, dd)))
        force.append(send(fx.at[up, :], dst.at[halo_s, :], at(-1, dd)))

    for copy in edges:
        copy.wait_recv()
    tall = rows + 2 * width
    spot = lax.broadcasted_iota(jnp.int32, (tall, 128), 0) + row * rows - width
    lanes = lax.broadcasted_iota(jnp.int32, (tall, 128), 1)
    inside = (spot >= 0) & (spot < rows_n * rows)
    is_e = lanes < width
    is_w = lanes >= 128 - width
    side_in = inside & ((is_e & (me < n - 1)) | (is_w & (me > 0)))
    west, east = h_w[...], h_e[...]

    def side(p):
        from_e = pltpu.roll(east, (128 - width * p) % 128, 1)
        from_w = pltpu.roll(west, (256 - width - width * p) % 128, 1)
        return jnp.where(is_e, from_e, from_w)

    def extend(middle, p, other):
        return (
            jnp.where(inside, middle, other),
            jnp.where(side_in, side(p), other),
        )

    coefs = [extend(cx[k], k, 1.0) for k in range(9)]
    mask = extend(wx[...].astype(F32), 9, 0.0)
    eta2 = extend(ex[...], 10, 0.0)
    for h in range(2):
        scale = mask[h] / functools.reduce(lambda a, b: a + b, [c[h] for c in coefs])
        for k in range(9):
            nrm[k, :, h * 128:(h + 1) * 128] = coefs[k][h] * scale

    half = 2 * pairs

    def contract(d, first):
        for m in range(m_dev):
            if main:
                parts = [
                    rb[d, pl.ds(t * cdev * pairs + m * half, half), :] for t in range(tiles)
                ]
                h, l = split(jnp.concatenate(parts, axis=1) if tiles > 1 else parts[0])
                value = dot(h, lh[m, d]) + dot(h, ll[m, d]) + dot(l, lh[m, d])
                if first:
                    spec[m] = value
                else:
                    spec[m] += value
            elif first:
                spec[m] = jnp.zeros_like(spec[m])
        if tail:
            e = lax.rem(d, per)
            chunk = d // per
            for c in range(cdev):
                packed = rb[d, pl.ds(tiles * cdev * pairs + c * lev, lev), :]
                for v in range(vars_n):
                    turn = lax.rem((e - v) * slot + 128 * vars_n, 128)
                    moved = pltpu.roll(packed, turn, 1)
                    place = pl.ds(c * pairs + v * lev, lev)
                    here = (lane >= e * slot) & (lane < (e + 1) * slot)
                    xt[chunk, place, :] = jnp.where(here, moved, xt[chunk, place, :])

    if tail:
        xt[...] = jnp.zeros_like(xt)
    contract(me, True)

    for copy in force:
        copy.wait_recv()
    live = jnp.concatenate([mask[0], mask[1]], axis=1)
    sides = jnp.where(side_in, jnp.where(is_e, fl_e[...], fl_w[...]), 0.0)
    pull = live * (RATE * jnp.concatenate([jnp.where(inside, fx[...], 0.0), sides], axis=1))
    eta = jnp.concatenate([eta2[0], eta2[1]], axis=1)
    for step in range(SUBS):
        across = [pltpu.roll(eta, 1, 1), eta, pltpu.roll(eta, 255, 1)]
        total = pull
        for q in range(3):
            turned = [pltpu.roll(across[q], 1, 0), across[q], pltpu.roll(across[q], tall - 1, 0)]
            for p in range(3):
                total = total + nrm[3 * p + q] * turned[p]
        eta = total
    eta_out[...] = eta[width:width + rows, 0:128]

    for r in range(1, n):
        blocks[r - 1].wait_recv()
        contract(lax.rem(me + n - r, n), False)
    if tail:
        for chunk in range(xt.shape[0]):
            for m in range(m_dev):
                h, l = split(xt[chunk, m * half:(m + 1) * half, :])
                group = pl.ds(chunk * per, per)
                high = th[m, group].reshape(128, th.shape[-1])
                low = tl[m, group].reshape(128, tl.shape[-1])
                spec[m] += dot(h, high) + dot(h, low) + dot(l, high)
    for copy in remotes:
        copy.wait_send()


def body(fourier, legendre, eta_start, coefs, wet, src_index, regrid_weight):
    n = lax.axis_size("dom")
    subs_n = lax.axis_size("sub")
    rows_n = lax.axis_size("group") * subs_n
    la, vars_n, lev, cols = fourier.shape
    m_dev, lat, ndeg = legendre.shape
    rows, blk = eta_start.shape
    pairs = vars_n * lev
    main = la // 128 * 128
    tail = la - main
    slot = -(-tail // 16) * 16 if tail else 128
    while 128 % slot:
        slot += 16
    if tail:
        assert slot * vars_n <= 128 and n % (128 // slot) == 0
    chunks = max(1, n // (128 // slot))
    surface = fourier[:, 0, 0, :]
    count = la * cols // blk
    flux = surface.reshape(count, blk)
    pad = -(-count // 8) * 8
    flux = jnp.pad(flux, ((0, pad - count), (0, 0)))
    x = jnp.transpose(fourier, (1, 2, 3, 0)).reshape(pairs * cols, la)
    index = jnp.transpose(src_index.reshape(rows, 2), (1, 0))
    weight = regrid_weight.reshape(rows, 2, blk, blk)
    depth = main // 128 * 2 * m_dev * pairs + (2 * m_dev * lev if tail else 0)
    tall = rows + 2 * SUBS
    dims = (n, rows_n, subs_n, la, pairs, cols, lev, m_dev, rows, count, slot)
    sends = (n - 1) * 2 + 12 + 8
    any_ = pl.BlockSpec(memory_space=pl.ANY)
    vmem = pl.BlockSpec(memory_space=pltpu.VMEM)
    spec, eta = pl.pallas_call(
        functools.partial(kernel, dims),
        out_shape=(
            jax.ShapeDtypeStruct((m_dev, 2 * pairs, ndeg), F32),
            jax.ShapeDtypeStruct((rows, blk), F32),
        ),
        in_specs=[any_] * 5 + [pl.BlockSpec(memory_space=pltpu.SMEM)] + [any_] * 2,
        out_specs=(vmem, vmem),
        scratch_shapes=[
            pltpu.VMEM((-(-la // 128), pairs * cols, 128), F32),
            pltpu.VMEM((pairs * cols, max(tail, 8)), F32),
            pltpu.VMEM(legendre.shape, F32),
            pltpu.VMEM(weight.shape, F32),
            pltpu.VMEM((n * pad, blk), F32),
            pltpu.VMEM((n - 1, depth, 128), F32),
            pltpu.VMEM((n, depth, 128), F32),
            pltpu.VMEM((m_dev, n, max(main, 16), ndeg), BF16),
            pltpu.VMEM((m_dev, n, max(main, 16), ndeg), BF16),
            pltpu.VMEM((m_dev, n, slot, ndeg), BF16),
            pltpu.VMEM((m_dev, n, slot, ndeg), BF16),
            pltpu.VMEM((chunks, 2 * m_dev * pairs, 128), F32),
            pltpu.VMEM((9, tall, blk), F32),
            pltpu.VMEM((tall, blk), jnp.int32),
            pltpu.VMEM((tall, blk), F32),
            pltpu.VMEM((tall, blk), F32),
            pltpu.VMEM((tall, blk), F32),
            pltpu.VMEM((tall, blk), F32),
            pltpu.VMEM((rows, blk), F32),
            pltpu.VMEM((rows, blk), F32),
            pltpu.VMEM((tall, blk), F32),
            pltpu.VMEM((tall, blk), F32),
            pltpu.VMEM((9, tall, 2 * blk), F32),
            pltpu.SemaphoreType.DMA((8 + main // 128 + m_dev,)),
            pltpu.SemaphoreType.DMA((sends,)),
            pltpu.SemaphoreType.DMA((sends,)),
        ],
        compiler_params=pltpu.CompilerParams(collective_id=0, has_side_effects=True),
    )(x, legendre, eta_start, coefs, wet, index, weight, flux)
    spectral = spec.reshape(m_dev, 2, vars_n, lev, ndeg)
    return jnp.transpose(spectral, (0, 2, 3, 1, 4)), eta


def solution(mesh):
    placed = (
        P("dom", None, ("group", "sub"), None),
        P("dom", None, None),
        P(("group", "sub"), "dom"),
        P(None, ("group", "sub"), "dom"),
        P(("group", "sub"), "dom"),
        P(("group", "sub"), "dom", None),
        P(("group", "sub"), "dom", None, None, None),
    )
    return jax.shard_map(
        body,
        mesh=mesh,
        in_specs=placed,
        out_specs=(P("dom", None, ("group", "sub"), None, None), P(("group", "sub"), "dom")),
        check_vma=False,
    )
```

time: 96.3 us -> 32 us (0.33)
  the two profiles are of different devices: /device:TPU:0 before, /device:TPU:11 now
where the time goes in v1:
time: 32 us; the launch traced here: 31.7 us
  Pallas kernels  26.3 us (82%)
  local copies, waits for them, and re-layouts  4.81 us (15%)
  between operations  0.65 us (2%)
    pallas_call x1, Pallas kernels, body(): pl.pallas_call(functools.partial(kernel, dims), out_shape=(jax.ShapeDtype...  26.3 us
    reshape x1, local copies, waits for them, and re-layouts, body(): spectral = spec.reshape(m_dev, 2, vars_n, lev, ndeg)  1.95 us
    unnamed x1, local copies, waits for them, and re-layouts  1.29 us
    slice x2, local copies, waits for them, and re-layouts, body(): surface = fourier[:, 0, 0, :]  0.84 us

profile of v1, /device:TPU:11, one launch (start us, length us, event | category | flops | bytes accessed | tf_op | source)
XLA Modules:
  0.0 31.7 jit_solution(110098411246326455)
XLA Ops:
  0.6 0.7 %slice.3 = f32[288,1,1,16]{0,3,2,1:T(8,128)S(1)} slice(f32[288,4,8,16]{0,3,2,1:T(8,128)} %param.7), slice={[0:288], [0:1], [0:1], [0:16]} | slice | bytes 36864 | tf_op jit(solution)/shard_map/slice | solution.py:308
  1.4 0.1 copy.11
  1.5 0.1 reshape_squeeze.3
  1.6 0.6 %pad.4.fl_hbm = f32[40,128]{1,0:T(8,128)} pad(f32[36,128]{1,0:T(8,128)S(1)} %reshape_squeeze.3, f32[]{:T(128)} %constant.2.clone.1), padding=0_4x0_0 | pad | bytes 38916 | tf_op jit(solution)/shard_map/jit(_pad)/pad | solution.py:312
  2.2 26.3 %shard_map.86 = (f32[2,64,640]{2,1,0:T(8,128)}, f32[16,128]{1,0:T(8,128)}) custom-call(f32[512,288]{1,0:T(8,128)} %bitcast.16, f32[2,1152,640]{2,1,0:T(8,128)} %l_hbm.1, f32[16,128]{1,0:T(8,128)} %eta_hbm.1, f32[9,16,128]{2,1,0:T(8,128)} %coef_hbm.1, s32[16,128]{1,0:T(8,128)} %wet_hbm.1, s32[2,16]{1,0:T(2,128)} %bitcast.19, f32[16,2,128,128]{3,2,1,0:T(8,128)} %bitcast.15, ...), custom_call_target="tpu_custom_call" | custom-call | tf_op jit(solution)/shard_map/pallas_call | solution.py:322
  28.5 2.0 %copy.14 = f32[2,2,4,8,640]{4,1,3,2,0:T(2,128)} copy(f32[2,2,4,8,640]{4,3,2,1,0:T(8,128)} %bitcast.18) | data formatting | bytes 655360 | tf_op jit(solution)/shard_map/reshape | solution.py:360
  30.4 1.3 %copy.16 = f32[16,128]{1,0:T(8,128)} copy(f32[16,128]{1,0:T(8,128)} %get-tuple-element.9) | data formatting | bytes 16384

commit v2 on v1

--- a/solution.py
+++ b/solution.py
@@ -25,12 +25,16 @@
 
 def kernel(
     dims,
-    x_hbm, l_hbm, eta_hbm, coef_hbm, wet_hbm, idx, w_hbm, fl_hbm,
-    spec, eta_out,
-    xv, xr, lv, wv, flb, sb, rb, lh, ll, th, tl, xt, cx, wx, ex, fx, fl_w, fl_e, pk_w, pk_e, h_w, h_e, nrm,
+    *refs,
+):
+    x_hbm, l_hbm, eta_hbm, coef_hbm, wet_hbm, idx_hbm, w_hbm = refs[:7]
+    fl_hbm = refs[7] if dims[-1] else None
+    (
+    out, eta_out,
+    idx, acc, tr, xv, xr, lv, wv, flb, sb, rb, lh, ll, th, tl, xt, cx, wx, ex, fx, fl_w, fl_e, pk_w, pk_e, h_w, h_e, nrm,
     lsem, ssem, rsem,
-):
-    n, rows_n, subs_n, la, pairs, cols, lev, m_dev, rows, count, slot = dims
+    ) = refs[7 + dims[-1]:]
+    n, rows_n, subs_n, la, pairs, cols, lev, m_dev, rows, count, slot, given = dims
     width = SUBS
     main = la // 128 * 128
     tail = la - main
@@ -60,15 +64,38 @@
 
     remotes = []
 
-    def send(src, dst, target):
+    def send(src, dst, target, ddom=0):
         i = len(remotes)
         copy = pltpu.make_async_remote_copy(
             src_ref=src, dst_ref=dst, send_sem=ssem.at[i], recv_sem=rsem.at[i],
             device_id=target, device_id_type=MESH,
         )
-        remotes.append(copy)
-        copy.start()
-        return copy
+        go = {1: me < n - 1, -1: me > 0}.get(ddom)
+        come = {1: me > 0, -1: me < n - 1}.get(ddom)
+        remotes.append((copy, go))
+        if go is None:
+            copy.start()
+        else:
+            pl.when(go)(copy.start)
+        return copy, come
+
+    def arrive(sent):
+        copy, come = sent
+        if come is None:
+            copy.wait_recv()
+        else:
+            pl.when(come)(copy.wait_recv)
+
+    def partner(r):
+        if n & (n - 1):
+            return lax.rem(me + r, n), lax.rem(me + n - r, n)
+        other = me
+        bit = 1
+        while bit < n:
+            if r & bit:
+                other = other + bit - 2 * bit * lax.rem(me // bit, 2)
+            bit *= 2
+        return other, other
 
     barrier = pltpu.get_barrier_semaphore()
     greet = [at(0, r) for r in range(1, n)]
@@ -82,8 +109,8 @@
     if tail:
         get_x.append(fetch(x_hbm.at[:, pl.ds(main, tail)], xr))
     mine = pl.ds(pl.multiple_of(me * pad, 8), pad)
-    get_f = fetch(fl_hbm, flb.at[mine, :])
-    get_r = fetch(w_hbm, wv)
+    get_f = fetch(fl_hbm, flb.at[mine, :]) if given else None
+    get_r = [fetch(idx_hbm, idx), fetch(w_hbm, wv)]
     get_l = [fetch(l_hbm.at[m], lv.at[m]) for m in range(m_dev)]
 
     lane = lax.broadcasted_iota(jnp.int32, (1, 128), 1)
@@ -101,27 +128,22 @@
     pk_w[...] = left
     pk_e[...] = right
 
-    pl.semaphore_wait(barrier, len(greet))
-    top, bottom = pl.ds(0, width), pl.ds(rows - width, width)
-    halo_n, halo_s = pl.ds(0, width), pl.ds(width + rows, width)
-    get_flux = [send(fl_hbm, flb.at[mine, :], at(0, r)) for r in range(1, n)]
-    edges = []
-    for src, dst in ((coef_hbm, cx), ):
-        edges.append(send(src.at[:, bottom, :], dst.at[:, halo_n, :], at(1, 0)))
-        edges.append(send(src.at[:, top, :], dst.at[:, halo_s, :], at(-1, 0)))
-    for src, dst in ((wet_hbm, wx), (eta_hbm, ex)):
-        edges.append(send(src.at[bottom, :], dst.at[halo_n, :], at(1, 0)))
-        edges.append(send(src.at[top, :], dst.at[halo_s, :], at(-1, 0)))
-    for src, dst, dd in ((pk_e, h_w, 1), (pk_w, h_e, -1)):
-        edges.append(send(src, dst.at[own, :], at(0, dd)))
-        edges.append(send(src.at[bottom, :], dst.at[halo_n, :], at(1, dd)))
-        edges.append(send(src.at[top, :], dst.at[halo_s, :], at(-1, dd)))
-
     for copy in get_x:
         copy.wait()
     vars_n = pairs // lev
     if tail:
         xv[tiles] = jnp.concatenate([xr[...], jnp.zeros((xr.shape[0], 128 - tail), F32)], axis=1)
+    if given:
+        get_f.wait()
+    else:
+        group = 128 // cols
+        for t in range(xv.shape[0]):
+            plane = jnp.concatenate([xv[t, 0:cols, :], jnp.zeros((128 - cols, 128), F32)], axis=0)
+            tr[t * 128:(t + 1) * 128, :] = plane.T
+        flux = tr[pl.ds(0, pad, stride=group), :]
+        for g in range(1, group):
+            flux = flux + pltpu.roll(tr[pl.ds(g, pad, stride=group), :], cols * g, 1)
+        flb[mine, :] = flux
 
     def pack(dest, store):
         for c in range(cdev):
@@ -143,12 +165,35 @@
             buffer[which, pl.ds(first, height), :] = value
         return store
 
-    blocks = []
-    for r in range(1, n):
-        dest = lax.rem(me + r, n)
-        pack(dest, keep(sb, r - 1))
-        blocks.append(send(sb.at[r - 1], rb.at[me], at(0, r)))
+    order = sorted(range(1, n), key=lambda r: (r < n // 2, r))
+    for r in order:
+        pack(partner(r)[0], keep(sb, r - 1))
     pack(me, keep(rb, me))
+    blocks = {}
+
+    def send_block(r):
+        blocks[r] = send(sb.at[r - 1], rb.at[me], at_dom(partner(r)[0]))
+
+    def at_dom(other):
+        return {"dom": other}
+
+    pl.semaphore_wait(barrier, len(greet))
+    top, bottom = pl.ds(0, width), pl.ds(rows - width, width)
+    halo_n, halo_s = pl.ds(0, width), pl.ds(width + rows, width)
+    get_flux = [send(flb.at[mine, :], flb.at[mine, :], at_dom(partner(r)[0])) for r in order]
+    edges = []
+    for src, dst in ((coef_hbm, cx), ):
+        edges.append(send(src.at[:, bottom, :], dst.at[:, halo_n, :], at(1, 0)))
+        edges.append(send(src.at[:, top, :], dst.at[:, halo_s, :], at(-1, 0)))
+    for src, dst in ((wet_hbm, wx), (eta_hbm, ex)):
+        edges.append(send(src.at[bottom, :], dst.at[halo_n, :], at(1, 0)))
+        edges.append(send(src.at[top, :], dst.at[halo_s, :], at(-1, 0)))
+    for src, dst, dd in ((pk_e, h_w, 1), (pk_w, h_e, -1)):
+        edges.append(send(src, dst.at[own, :], at(0, dd), dd))
+        edges.append(send(src.at[bottom, :], dst.at[halo_n, :], at(1, dd), dd))
+        edges.append(send(src.at[top, :], dst.at[halo_s, :], at(-1, dd), dd))
+
+    send_block(order[0])
 
     for copy in get_l:
         copy.wait()
@@ -171,10 +216,10 @@
 
     lax.fori_loop(0, n, split_legendre, 0)
 
-    get_f.wait()
     for copy in get_flux:
-        copy.wait_recv()
-    get_r.wait()
+        arrive(copy)
+    for copy in get_r:
+        copy.wait()
 
     def regrid(i, total):
         part = None
@@ -192,12 +237,15 @@
     force.append(send(fx.at[down, :], fx.at[halo_n, :], at(1, 0)))
     force.append(send(fx.at[up, :], fx.at[halo_s, :], at(-1, 0)))
     for dst, dd in ((fl_w, 1), (fl_e, -1)):
-        force.append(send(fx.at[own, :], dst.at[own, :], at(0, dd)))
-        force.append(send(fx.at[down, :], dst.at[halo_n, :], at(1, dd)))
-        force.append(send(fx.at[up, :], dst.at[halo_s, :], at(-1, dd)))
+        force.append(send(fx.at[own, :], dst.at[own, :], at(0, dd), dd))
+        force.append(send(fx.at[down, :], dst.at[halo_n, :], at(1, dd), dd))
+        force.append(send(fx.at[up, :], dst.at[halo_s, :], at(-1, dd), dd))
+
+    for r in order[1:]:
+        send_block(r)
 
     for copy in edges:
-        copy.wait_recv()
+        arrive(copy)
     tall = rows + 2 * width
     spot = lax.broadcasted_iota(jnp.int32, (tall, 128), 0) + row * rows - width
     lanes = lax.broadcasted_iota(jnp.int32, (tall, 128), 1)
@@ -237,11 +285,11 @@
                 h, l = split(jnp.concatenate(parts, axis=1) if tiles > 1 else parts[0])
                 value = dot(h, lh[m, d]) + dot(h, ll[m, d]) + dot(l, lh[m, d])
                 if first:
-                    spec[m] = value
+                    acc[m] = value
                 else:
-                    spec[m] += value
+                    acc[m] += value
             elif first:
-                spec[m] = jnp.zeros_like(spec[m])
+                acc[m] = jnp.zeros_like(acc[m])
         if tail:
             e = lax.rem(d, per)
             chunk = d // per
@@ -259,7 +307,7 @@
     contract(me, True)
 
     for copy in force:
-        copy.wait_recv()
+        arrive(copy)
     live = jnp.concatenate([mask[0], mask[1]], axis=1)
     sides = jnp.where(side_in, jnp.where(is_e, fl_e[...], fl_w[...]), 0.0)
     pull = live * (RATE * jnp.concatenate([jnp.where(inside, fx[...], 0.0), sides], axis=1))
@@ -274,9 +322,9 @@
         eta = total
     eta_out[...] = eta[width:width + rows, 0:128]
 
-    for r in range(1, n):
-        blocks[r - 1].wait_recv()
-        contract(lax.rem(me + n - r, n), False)
+    for r in order[:1] + order[:0:-1]:
+        arrive(blocks[r])
+        contract(partner(r)[1], False)
     if tail:
         for chunk in range(xt.shape[0]):
             for m in range(m_dev):
@@ -284,9 +332,25 @@
                 group = pl.ds(chunk * per, per)
                 high = th[m, group].reshape(128, th.shape[-1])
                 low = tl[m, group].reshape(128, tl.shape[-1])
-                spec[m] += dot(h, high) + dot(h, low) + dot(l, high)
-    for copy in remotes:
-        copy.wait_send()
+                acc[m] += dot(h, high) + dot(h, low) + dot(l, high)
+    for m in range(m_dev):
+        for v in range(vars_n):
+            for r in range(2):
+                out[m, v, :, r, :] = acc[m, pl.ds((r * vars_n + v) * lev, lev), :]
+    for copy, go in remotes:
+        if go is None:
+            copy.wait_send()
+        else:
+            pl.when(go)(copy.wait_send)
+
+
+def finish(spec_in, eta_in, spec_out, eta_out, sem):
+    first = pltpu.make_async_copy(spec_in, spec_out, sem.at[0])
+    second = pltpu.make_async_copy(eta_in, eta_out, sem.at[1])
+    first.start()
+    second.start()
+    first.wait()
+    second.wait()
 
 
 def body(fourier, legendre, eta_start, coefs, wet, src_index, regrid_weight):
@@ -305,29 +369,38 @@
     if tail:
         assert slot * vars_n <= 128 and n % (128 // slot) == 0
     chunks = max(1, n // (128 // slot))
-    surface = fourier[:, 0, 0, :]
     count = la * cols // blk
-    flux = surface.reshape(count, blk)
     pad = -(-count // 8) * 8
-    flux = jnp.pad(flux, ((0, pad - count), (0, 0)))
+    given = int(blk % cols != 0 or la % (blk // cols) != 0)
+    more = []
+    if given:
+        flux = fourier[:, 0, 0, :].reshape(count, blk)
+        more = [jnp.pad(flux, ((0, pad - count), (0, 0)))]
     x = jnp.transpose(fourier, (1, 2, 3, 0)).reshape(pairs * cols, la)
     index = jnp.transpose(src_index.reshape(rows, 2), (1, 0))
     weight = regrid_weight.reshape(rows, 2, blk, blk)
     depth = main // 128 * 2 * m_dev * pairs + (2 * m_dev * lev if tail else 0)
     tall = rows + 2 * SUBS
-    dims = (n, rows_n, subs_n, la, pairs, cols, lev, m_dev, rows, count, slot)
+    dims = (n, rows_n, subs_n, la, pairs, cols, lev, m_dev, rows, count, slot, given)
     sends = (n - 1) * 2 + 12 + 8
-    any_ = pl.BlockSpec(memory_space=pl.ANY)
+    any_ = pl.BlockSpec(memory_space=pltpu.HBM)
     vmem = pl.BlockSpec(memory_space=pltpu.VMEM)
+    held = [
+        pltpu.with_memory_space_constraint(a, pltpu.HBM)
+        for a in (x, legendre, eta_start, coefs, wet, index, weight, *more)
+    ]
     spec, eta = pl.pallas_call(
         functools.partial(kernel, dims),
         out_shape=(
-            jax.ShapeDtypeStruct((m_dev, 2 * pairs, ndeg), F32),
+            jax.ShapeDtypeStruct((m_dev, vars_n, lev, 2, ndeg), F32),
             jax.ShapeDtypeStruct((rows, blk), F32),
         ),
-        in_specs=[any_] * 5 + [pl.BlockSpec(memory_space=pltpu.SMEM)] + [any_] * 2,
+        in_specs=[any_] * (7 + given),
         out_specs=(vmem, vmem),
         scratch_shapes=[
+            pltpu.SMEM((2, rows), jnp.int32),
+            pltpu.VMEM((m_dev, 2 * pairs, ndeg), F32),
+            pltpu.VMEM((-(-la // 128) * 128, 128), F32),
             pltpu.VMEM((-(-la // 128), pairs * cols, 128), F32),
             pltpu.VMEM((pairs * cols, max(tail, 8)), F32),
             pltpu.VMEM(legendre.shape, F32),
@@ -351,14 +424,26 @@
             pltpu.VMEM((tall, blk), F32),
             pltpu.VMEM((tall, blk), F32),
             pltpu.VMEM((9, tall, 2 * blk), F32),
-            pltpu.SemaphoreType.DMA((8 + main // 128 + m_dev,)),
+            pltpu.SemaphoreType.DMA((9 + main // 128 + m_dev,)),
             pltpu.SemaphoreType.DMA((sends,)),
             pltpu.SemaphoreType.DMA((sends,)),
         ],
-        compiler_params=pltpu.CompilerParams(collective_id=0, has_side_effects=True),
-    )(x, legendre, eta_start, coefs, wet, index, weight, flux)
-    spectral = spec.reshape(m_dev, 2, vars_n, lev, ndeg)
-    return jnp.transpose(spectral, (0, 2, 3, 1, 4)), eta
+        compiler_params=pltpu.CompilerParams(
+            collective_id=0, has_side_effects=True, vmem_limit_bytes=32 * 1024 * 1024
+        ),
+    )(*held)
+    spec, eta = pl.pallas_call(
+        finish,
+        out_shape=(
+            jax.ShapeDtypeStruct(spec.shape, F32),
+            jax.ShapeDtypeStruct(eta.shape, F32),
+        ),
+        in_specs=[vmem, vmem],
+        out_specs=(any_, any_),
+        scratch_shapes=[pltpu.SemaphoreType.DMA((2,))],
+        compiler_params=pltpu.CompilerParams(vmem_limit_bytes=2 * 1024 * 1024),
+    )(spec, eta)
+    return spec, eta
 
 
 def solution(mesh):

time: 32 us -> 25.5 us (0.80)
  the two profiles are of different devices: /device:TPU:11 before, /device:TPU:0 now
where the time goes in v2:
time: 25.5 us; the launch traced here: 25.4 us
  Pallas kernels  24.7 us (97%)
  between operations  0.64 us (3%)
    pallas_call x1, Pallas kernels, body(): pl.pallas_call(functools.partial(kernel, dims), out_shape=(jax.ShapeDtype...  24 us
    pallas_call x1, Pallas kernels, body(): pl.pallas_call(finish, out_shape=(jax.ShapeDtypeStruct(spec.shape, F32),...  0.75 us

profile of v2, /device:TPU:0, one launch (start us, length us, event | category | flops | bytes accessed | tf_op | source)
XLA Modules:
  0.0 25.4 jit_solution(4587109435581577150)
XLA Ops:
  0.6 24.0 %shard_map.86 = (f32[2,4,8,2,640]{4,3,2,1,0:T(2,128)S(1)}, f32[16,128]{1,0:T(8,128)S(1)}) custom-call(f32[512,288]{1,0:T(8,128)} %bitcast.8, f32[2,1152,640]{2,1,0:T(8,128)} %refs_1_.1, f32[16,128]{1,0:T(8,128)} %refs_2_.1, f32[9,16,128]{2,1,0:T(8,128)} %refs_3_.1, s32[16,128]{1,0:T(8,128)} %refs_4_.1, s32[2,16]{1,0:T(2,128)} %bitcast.9, ...), custom_call_target="tpu_custom_call" | custom-call | tf_op jit(solution)/shard_map/pallas_call | solution.py:392
  24.6 0.7 %shard_map.87 = (f32[2,4,8,2,640]{4,3,2,1,0:T(2,128)}, f32[16,128]{1,0:T(8,128)}) custom-call(f32[2,4,8,2,640]{4,3,2,1,0:T(2,128)S(1)} %get-tuple-element.4.spec_in, f32[16,128]{1,0:T(8,128)S(1)} %get-tuple-element.5.eta_in), custom_call_target="tpu_custom_call" | custom-call | tf_op jit(solution)/shard_map/pallas_call | solution.py:435

commit v3 on v2

--- a/solution.py
+++ b/solution.py
@@ -169,10 +169,16 @@
     for r in order:
         pack(partner(r)[0], keep(sb, r - 1))
     pack(me, keep(rb, me))
-    blocks = {}
-
-    def send_block(r):
-        blocks[r] = send(sb.at[r - 1], rb.at[me], at_dom(partner(r)[0]))
+    blocks = {r: [] for r in order}
+    depth = sb.shape[1]
+    cut = depth // 16 * 8
+    head, rear = pl.ds(0, cut), pl.ds(cut, depth - cut)
+
+    def send_block(r, *parts):
+        for part in parts:
+            blocks[r].append(
+                send(sb.at[r - 1, part, :], rb.at[me, part, :], at_dom(partner(r)[0]))
+            )
 
     def at_dom(other):
         return {"dom": other}
@@ -180,7 +186,11 @@
     pl.semaphore_wait(barrier, len(greet))
     top, bottom = pl.ds(0, width), pl.ds(rows - width, width)
     halo_n, halo_s = pl.ds(0, width), pl.ds(width + rows, width)
-    get_flux = [send(flb.at[mine, :], flb.at[mine, :], at_dom(partner(r)[0])) for r in order]
+    relay = n == 4
+    get_flux = [
+        send(flb.at[mine, :], flb.at[mine, :], at_dom(partner(r)[0]))
+        for r in order if r < 3 or not relay
+    ]
     edges = []
     for src, dst in ((coef_hbm, cx), ):
         edges.append(send(src.at[:, bottom, :], dst.at[:, halo_n, :], at(1, 0)))
@@ -193,7 +203,8 @@
         edges.append(send(src.at[bottom, :], dst.at[halo_n, :], at(1, dd), dd))
         edges.append(send(src.at[top, :], dst.at[halo_s, :], at(-1, dd), dd))
 
-    send_block(order[0])
+    send_block(order[0], head, rear)
+    send_block(order[1], head)
 
     for copy in get_l:
         copy.wait()
@@ -214,7 +225,12 @@
                 tl[m, d] = l
         return carry
 
-    lax.fori_loop(0, n, split_legendre, 0)
+    lax.fori_loop(0, n // 2, split_legendre, 0)
+    if relay:
+        arrive(get_flux[0])
+        across = pl.ds(pl.multiple_of(partner(2)[0] * pad, 8), pad)
+        get_flux = get_flux[1:] + [send(flb.at[across, :], flb.at[across, :], at_dom(partner(1)[0]))]
+    lax.fori_loop(n // 2, n, split_legendre, 0)
 
     for copy in get_flux:
         arrive(copy)
@@ -241,8 +257,9 @@
         force.append(send(fx.at[down, :], dst.at[halo_n, :], at(1, dd), dd))
         force.append(send(fx.at[up, :], dst.at[halo_s, :], at(-1, dd), dd))
 
-    for r in order[1:]:
-        send_block(r)
+    send_block(order[1], rear)
+    for r in order[2:]:
+        send_block(r, head, rear)
 
     for copy in edges:
         arrive(copy)
@@ -306,6 +323,13 @@
         xt[...] = jnp.zeros_like(xt)
     contract(me, True)
 
+    def receive(r):
+        for part in blocks[r]:
+            arrive(part)
+        contract(partner(r)[1], False)
+
+    receive(order[0])
+
     for copy in force:
         arrive(copy)
     live = jnp.concatenate([mask[0], mask[1]], axis=1)
@@ -322,9 +346,8 @@
         eta = total
     eta_out[...] = eta[width:width + rows, 0:128]
 
-    for r in order[:1] + order[:0:-1]:
-        arrive(blocks[r])
-        contract(partner(r)[1], False)
+    for r in order[:0:-1]:
+        receive(r)
     if tail:
         for chunk in range(xt.shape[0]):
             for m in range(m_dev):
@@ -382,7 +405,7 @@
     depth = main // 128 * 2 * m_dev * pairs + (2 * m_dev * lev if tail else 0)
     tall = rows + 2 * SUBS
     dims = (n, rows_n, subs_n, la, pairs, cols, lev, m_dev, rows, count, slot, given)
-    sends = (n - 1) * 2 + 12 + 8
+    sends = (n - 1) * 3 + 12 + 8
     any_ = pl.BlockSpec(memory_space=pltpu.HBM)
     vmem = pl.BlockSpec(memory_space=pltpu.VMEM)
     held = [

time: 25.5 us -> 25.1 us (0.984)
  Pallas kernels: 24.7 us -> 24.3 us
    pallas_call x1, Pallas kernels: 24 us -> 23.5 us  [body(): pl.pallas_call(functools.partial(kernel, dims), out_shape=(jax.ShapeDtype...]
where the time goes in v3:
time: 25.1 us; the launch traced here: 24.9 us
  Pallas kernels  24.3 us (97%)
  between operations  0.64 us (3%)
    pallas_call x1, Pallas kernels, body(): pl.pallas_call(functools.partial(kernel, dims), out_shape=(jax.ShapeDtype...  23.5 us
    pallas_call x1, Pallas kernels, body(): pl.pallas_call(finish, out_shape=(jax.ShapeDtypeStruct(spec.shape, F32),...  0.75 us

profile of v3, /device:TPU:0, one launch (start us, length us, event | category | flops | bytes accessed | tf_op | source)
XLA Modules:
  0.0 24.9 jit_solution(3302009321961786936)
XLA Ops:
  0.6 23.5 %shard_map.86 = (f32[2,4,8,2,640]{4,3,2,1,0:T(2,128)S(1)}, f32[16,128]{1,0:T(8,128)S(1)}) custom-call(f32[512,288]{1,0:T(8,128)} %bitcast.8, f32[2,1152,640]{2,1,0:T(8,128)} %refs_1_.1, f32[16,128]{1,0:T(8,128)} %refs_2_.1, f32[9,16,128]{2,1,0:T(8,128)} %refs_3_.1, s32[16,128]{1,0:T(8,128)} %refs_4_.1, s32[2,16]{1,0:T(2,128)} %bitcast.9, ...), custom_call_target="tpu_custom_call" | custom-call | tf_op jit(solution)/shard_map/pallas_call | solution.py:415
  24.2 0.7 %shard_map.87 = (f32[2,4,8,2,640]{4,3,2,1,0:T(2,128)}, f32[16,128]{1,0:T(8,128)}) custom-call(f32[2,4,8,2,640]{4,3,2,1,0:T(2,128)S(1)} %get-tuple-element.4.spec_in, f32[16,128]{1,0:T(8,128)S(1)} %get-tuple-element.5.eta_in), custom_call_target="tpu_custom_call" | custom-call | tf_op jit(solution)/shard_map/pallas_call | solution.py:458

commit v4 on v3

--- a/solution.py
+++ b/solution.py
@@ -97,6 +97,9 @@
             bit *= 2
         return other, other
 
+    get_x = [fetch(x_hbm.at[:, pl.ds(t * 128, 128)], xv.at[t]) for t in range(tiles)]
+    if tail:
+        get_x.append(fetch(x_hbm.at[:, pl.ds(main, tail)], xr))
     barrier = pltpu.get_barrier_semaphore()
     greet = [at(0, r) for r in range(1, n)]
     greet += [at(dr, dd) for dr in (-1, 1) for dd in (-1, 0, 1)]
@@ -105,13 +108,8 @@
     get_c = fetch(coef_hbm, cx.at[:, pl.ds(width, rows), :])
     get_w = fetch(wet_hbm, wx.at[pl.ds(width, rows), :])
     get_e = fetch(eta_hbm, ex.at[pl.ds(width, rows), :])
-    get_x = [fetch(x_hbm.at[:, pl.ds(t * 128, 128)], xv.at[t]) for t in range(tiles)]
-    if tail:
-        get_x.append(fetch(x_hbm.at[:, pl.ds(main, tail)], xr))
     mine = pl.ds(pl.multiple_of(me * pad, 8), pad)
     get_f = fetch(fl_hbm, flb.at[mine, :]) if given else None
-    get_r = [fetch(idx_hbm, idx), fetch(w_hbm, wv)]
-    get_l = [fetch(l_hbm.at[m], lv.at[m]) for m in range(m_dev)]
 
     lane = lax.broadcasted_iota(jnp.int32, (1, 128), 1)
     get_c.wait()
@@ -130,6 +128,8 @@
 
     for copy in get_x:
         copy.wait()
+    get_r = [fetch(idx_hbm, idx), fetch(w_hbm, wv)]
+    get_l = [fetch(l_hbm.at[m], lv.at[m]) for m in range(m_dev)]
     vars_n = pairs // lev
     if tail:
         xv[tiles] = jnp.concatenate([xr[...], jnp.zeros((xr.shape[0], 128 - tail), F32)], axis=1)
@@ -166,9 +166,7 @@
         return store
 
     order = sorted(range(1, n), key=lambda r: (r < n // 2, r))
-    for r in order:
-        pack(partner(r)[0], keep(sb, r - 1))
-    pack(me, keep(rb, me))
+    pack(partner(order[0])[0], keep(sb, order[0] - 1))
     blocks = {r: [] for r in order}
     depth = sb.shape[1]
     cut = depth // 16 * 8
@@ -186,10 +184,9 @@
     pl.semaphore_wait(barrier, len(greet))
     top, bottom = pl.ds(0, width), pl.ds(rows - width, width)
     halo_n, halo_s = pl.ds(0, width), pl.ds(width + rows, width)
-    relay = n == 4
     get_flux = [
         send(flb.at[mine, :], flb.at[mine, :], at_dom(partner(r)[0]))
-        for r in order if r < 3 or not relay
+        for r in order
     ]
     edges = []
     for src, dst in ((coef_hbm, cx), ):
@@ -204,7 +201,10 @@
         edges.append(send(src.at[top, :], dst.at[halo_s, :], at(-1, dd), dd))
 
     send_block(order[0], head, rear)
+    for r in order[1:]:
+        pack(partner(r)[0], keep(sb, r - 1))
     send_block(order[1], head)
+    pack(me, keep(rb, me))
 
     for copy in get_l:
         copy.wait()
@@ -225,12 +225,7 @@
                 tl[m, d] = l
         return carry
 
-    lax.fori_loop(0, n // 2, split_legendre, 0)
-    if relay:
-        arrive(get_flux[0])
-        across = pl.ds(pl.multiple_of(partner(2)[0] * pad, 8), pad)
-        get_flux = get_flux[1:] + [send(flb.at[across, :], flb.at[across, :], at_dom(partner(1)[0]))]
-    lax.fori_loop(n // 2, n, split_legendre, 0)
+    lax.fori_loop(0, n, split_legendre, 0)
 
     for copy in get_flux:
         arrive(copy)
@@ -246,7 +241,7 @@
             part = term if part is None else part + term
         return jnp.where(lane == i, jnp.sum(part, axis=1, keepdims=True), total)
 
-    forced = lax.fori_loop(0, rows, regrid, jnp.zeros((128, 128), F32))
+    forced = lax.fori_loop(0, rows, regrid, jnp.zeros((128, 128), F32), unroll=4)
     fx[own, :] = forced.T[0:rows]
     up, down = pl.ds(width, width), pl.ds(rows, width)
     force = []

time: 25.1 us -> 24.7 us (0.984)
  Pallas kernels: 24.3 us -> 23.8 us
    pallas_call x1, Pallas kernels: 23.5 us -> 23.1 us  [body(): pl.pallas_call(functools.partial(kernel, dims), out_shape=(jax.ShapeDtype...]
where the time goes in v4:
time: 24.7 us; the launch traced here: 24.5 us
  Pallas kernels  23.8 us (96%)
  between operations  0.64 us (3%)
    pallas_call x1, Pallas kernels, body(): pl.pallas_call(functools.partial(kernel, dims), out_shape=(jax.ShapeDtype...  23.1 us
    pallas_call x1, Pallas kernels, body(): pl.pallas_call(finish, out_shape=(jax.ShapeDtypeStruct(spec.shape, F32),...  0.75 us

profile of v4, /device:TPU:0, one launch (start us, length us, event | category | flops | bytes accessed | tf_op | source)
XLA Modules:
  0.0 24.5 jit_solution(9227539378694411073)
XLA Ops:
  0.6 23.1 %shard_map.86 = (f32[2,4,8,2,640]{4,3,2,1,0:T(2,128)S(1)}, f32[16,128]{1,0:T(8,128)S(1)}) custom-call(f32[512,288]{1,0:T(8,128)} %bitcast.8, f32[2,1152,640]{2,1,0:T(8,128)} %refs_1_.1, f32[16,128]{1,0:T(8,128)} %refs_2_.1, f32[9,16,128]{2,1,0:T(8,128)} %refs_3_.1, s32[16,128]{1,0:T(8,128)} %refs_4_.1, s32[2,16]{1,0:T(2,128)} %bitcast.9, ...), custom_call_target="tpu_custom_call" | custom-call | tf_op jit(solution)/shard_map/pallas_call | solution.py:410
  23.7 0.7 %shard_map.87 = (f32[2,4,8,2,640]{4,3,2,1,0:T(2,128)}, f32[16,128]{1,0:T(8,128)}) custom-call(f32[2,4,8,2,640]{4,3,2,1,0:T(2,128)S(1)} %get-tuple-element.4.spec_in, f32[16,128]{1,0:T(8,128)S(1)} %get-tuple-element.5.eta_in), custom_call_target="tpu_custom_call" | custom-call | tf_op jit(solution)/shard_map/pallas_call | solution.py:453
